TPU v7x, 32 devices: a whole 2x2x4 slice. The times are simulated.
32 devices in a mesh: fsdp: 8 (over z, x), seq: 4 (over y, core).
Axes of the slice: x: 2, y: 2, z: 4, core: 2. Of those that a mesh axis runs over, the one named last changes fastest.
Arguments:
- residual: bfloat16 [24, 1024, 767], P('fsdp', 'seq'), may hold values from -6 to 6
- out_grad: bfloat16 [24, 1024, 767], P('fsdp', 'seq'), may hold values from -6 to 6
- doc_lengths: int32 [24, 8], P('fsdp'), may hold values from 1 to 512, 1024 in all within a row
- gain_one: float32 [768], replicated, may hold values from 0.5 to 1.5
- qkv_weight: float32 [768, 2304], P('fsdp'), may hold values from -0.21875 to 0.21875
- qv_bias: float32 [12, 128], replicated, may hold values from -3 to 3
- out_weight: float32 [768, 767], P('fsdp'), may hold values from -0.875 to 0.875
- out_bias: float32 [767], replicated, may hold values from -3 to 3
- gain_two: float32 [768], replicated, may hold values from 0.5 to 1.5
- fc_weight: float32 [768, 3072], P('fsdp'), may hold values from -0.21875 to 0.21875
- fc_bias: float32 [3072], replicated, may hold values from -3 to 3
- proj_weight: float32 [3072, 767], P('fsdp'), may hold values from -0.15625 to 0.15625
- proj_bias: float32 [767], replicated, may hold values from -3 to 3
Outputs:
- output: bfloat16 [24, 1024, 767], P('fsdp', 'seq')
- input_grad: float32 [24, 1024, 767], P('fsdp', 'seq')
- gain_one_grad: float32 [768], replicated
- qkv_weight_grad: float32 [768, 2304], P('fsdp')
- qv_bias_grad: float32 [12, 128], replicated
- out_weight_grad: float32 [768, 767], P('fsdp')
- out_bias_grad: float32 [767], replicated
- gain_two_grad: float32 [768], replicated
- fc_weight_grad: float32 [768, 3072], P('fsdp')
- fc_bias_grad: float32 [3072], replicated
- proj_weight_grad: float32 [3072, 767], P('fsdp')
- proj_bias_grad: float32 [767], replicated
Inputs may be any that keep to these rules, and one draw needn't show every extreme that they name: `doc_lengths`: each sequence's 8 document lengths sum to 1024; the longest is exactly 512 tokens.
All inputs are finite; a program needn't handle non-finite values.
Results may differ from a plain program's by a relative error of at most 0.014.
Values may be sent and summed in bfloat16 or wider, within the bound.
No kernel may reach another device: no remote copies, remote signals or barrier semaphores. Data moves between devices by JAX's collectives and lax.ppermute only.
A program may use at most 320 MiB of HBM per device.

v0:
```python
import functools
import jax
import jax.numpy as jnp
from jax import lax
from jax.sharding import PartitionSpec as P

EPS = 1e-06


def centred_norm(residual, gain):
    row_total = jnp.sum(residual, axis=-1, keepdims=True)
    full_row = jnp.concatenate([residual, -row_total], axis=-1)
    inv_rms = lax.rsqrt(jnp.mean(full_row * full_row, axis=-1, keepdims=True) + EPS)
    return full_row * inv_rms * gain


def document_index(lengths, length):
    starts = jnp.cumsum(lengths, axis=1) - lengths
    position = jnp.arange(length, dtype=jnp.int32)
    inside = (position[None, :, None] >= starts[:, None, :]).astype(jnp.int32)
    return jnp.sum(inside, axis=2) - 1


def masked_scores(queries, key_rows, doc_ids, first_row, row_count, factor):
    scores = factor * jnp.einsum(
        "bqhe,bkhe->bhqk", queries, key_rows, preferred_element_type=jnp.float32
    )
    length = key_rows.shape[1]
    row_pos = first_row + jnp.arange(row_count, dtype=jnp.int32)
    col_pos = jnp.arange(length, dtype=jnp.int32)
    row_ids = doc_ids[:, first_row : first_row + row_count]
    allowed = (row_ids[:, :, None] == doc_ids[:, None, :]) & (
        col_pos[None, None, :] <= row_pos[None, :, None]
    )
    return jnp.where(allowed[:, None], scores, -1e30)


def local(
    residual,
    out_grad,
    doc_lengths,
    gain_one,
    qkv_weight,
    qv_bias,
    out_weight,
    out_bias,
    gain_two,
    fc_weight,
    fc_bias,
    proj_weight,
    proj_bias,
):
    ranks = lax.axis_size("seq")
    seq_count, local_len, narrow = residual.shape
    width = narrow + 1
    full_len = local_len * ranks
    heads_all = qv_bias.shape[0]
    head_dim = qv_bias.shape[1] // 2
    my_heads = heads_all // ranks
    token_count = seq_count * local_len
    factor = head_dim ** (-0.5)
    block_rows = min(512, full_len)
    qkv_matrix, out_matrix, fc_matrix, proj_matrix = (
        lax.all_gather(qkv_weight.astype(jnp.bfloat16), "fsdp", axis=0, tiled=True),
        lax.all_gather(out_weight.astype(jnp.bfloat16), "fsdp", axis=0, tiled=True),
        lax.all_gather(fc_weight.astype(jnp.bfloat16), "fsdp", axis=0, tiled=True),
        lax.all_gather(proj_weight.astype(jnp.bfloat16), "fsdp", axis=0, tiled=True),
    )
    resid_flat = residual.astype(jnp.float32).reshape(token_count, narrow)
    normed_one = centred_norm(resid_flat, gain_one).astype(jnp.bfloat16)
    zero_part = jnp.zeros((heads_all, head_dim), jnp.float32)
    bias_full = jnp.stack(
        [qv_bias[:, :head_dim], zero_part, qv_bias[:, head_dim:]], axis=1
    ).reshape(3 * width)
    packed = (
        jnp.dot(normed_one, qkv_matrix, preferred_element_type=jnp.float32) + bias_full
    ).astype(jnp.bfloat16)
    packed = packed.reshape(seq_count, local_len, ranks, my_heads * 3 * head_dim)
    by_heads = lax.all_to_all(packed, "seq", split_axis=2, concat_axis=1, tiled=True)
    by_heads = by_heads.reshape(seq_count, full_len, my_heads, 3, head_dim)
    queries = by_heads[:, :, :, 0]
    key_rows = by_heads[:, :, :, 1]
    value_rows = by_heads[:, :, :, 2]
    doc_ids = document_index(doc_lengths, full_len)
    outputs_list = []
    lse_list = []
    for first_row in range(0, full_len, block_rows):
        scores = masked_scores(
            queries[:, first_row : first_row + block_rows],
            key_rows,
            doc_ids,
            first_row,
            block_rows,
            factor,
        )
        row_max = jnp.max(scores, axis=-1, keepdims=True)
        exp_scores = jnp.exp(scores - row_max)
        row_total = jnp.sum(exp_scores, axis=-1, keepdims=True)
        prob_low = (exp_scores / row_total).astype(jnp.bfloat16)
        lse_list.append(row_max + jnp.log(row_total))
        outputs_list.append(
            jnp.einsum("bhqk,bkhe->bqhe", prob_low, value_rows, preferred_element_type=jnp.float32)
        )
    attended = jnp.concatenate(outputs_list, axis=1).astype(jnp.bfloat16)
    attended = attended.reshape(seq_count, full_len, my_heads * head_dim)
    by_tokens = lax.all_to_all(attended, "seq", split_axis=1, concat_axis=2, tiled=True)
    attn_flat = by_tokens.reshape(token_count, width)
    middle = (
        resid_flat + jnp.dot(attn_flat, out_matrix, preferred_element_type=jnp.float32) + out_bias
    )
    normed_two = centred_norm(middle, gain_two).astype(jnp.bfloat16)
    pre_act = jnp.dot(normed_two, fc_matrix, preferred_element_type=jnp.float32) + fc_bias
    hidden = jax.nn.gelu(pre_act, approximate=True).astype(jnp.bfloat16)
    output = middle + jnp.dot(hidden, proj_matrix, preferred_element_type=jnp.float32) + proj_bias
    output = output.astype(jnp.bfloat16).reshape(seq_count, local_len, narrow)
    qkv_matrix, out_matrix, fc_matrix, proj_matrix = (
        lax.all_gather(qkv_weight.astype(jnp.bfloat16), "fsdp", axis=0, tiled=True),
        lax.all_gather(out_weight.astype(jnp.bfloat16), "fsdp", axis=0, tiled=True),
        lax.all_gather(fc_weight.astype(jnp.bfloat16), "fsdp", axis=0, tiled=True),
        lax.all_gather(proj_weight.astype(jnp.bfloat16), "fsdp", axis=0, tiled=True),
    )
    grad_low = out_grad.reshape(token_count, narrow)
    grad_flat = grad_low.astype(jnp.float32)
    proj_grad = jnp.einsum("tf,tc->fc", hidden, grad_low, preferred_element_type=jnp.float32)
    proj_bias_grad = jnp.sum(grad_flat, axis=0)
    d_hidden = jnp.einsum("tc,fc->tf", grad_low, proj_matrix, preferred_element_type=jnp.float32)
    gelu_value, gelu_back = jax.vjp(functools.partial(jax.nn.gelu, approximate=True), pre_act)
    d_pre = gelu_back(d_hidden)[0].astype(jnp.bfloat16)
    fc_grad = jnp.einsum("td,tf->df", normed_two, d_pre, preferred_element_type=jnp.float32)
    fc_bias_grad = jnp.sum(d_pre.astype(jnp.float32), axis=0)
    d_norm_two = jnp.einsum("tf,df->td", d_pre, fc_matrix, preferred_element_type=jnp.float32)
    second_value, second_back = jax.vjp(centred_norm, middle, gain_two)
    d_mid_part, gain_two_grad = second_back(d_norm_two)
    d_middle = grad_flat + d_mid_part
    d_branch = d_middle.astype(jnp.bfloat16)
    out_weight_part = jnp.einsum(
        "td,tc->dc", attn_flat, d_branch, preferred_element_type=jnp.float32
    )
    out_bias_grad = jnp.sum(d_branch.astype(jnp.float32), axis=0)
    d_attn = jnp.einsum(
        "tc,dc->td", d_branch, out_matrix, preferred_element_type=jnp.float32
    ).astype(jnp.bfloat16)
    d_attn = d_attn.reshape(seq_count, local_len, ranks, my_heads * head_dim)
    d_heads = lax.all_to_all(d_attn, "seq", split_axis=2, concat_axis=1, tiled=True)
    d_heads = d_heads.reshape(seq_count, full_len, my_heads, head_dim)
    key_grad = jnp.zeros((seq_count, full_len, my_heads, head_dim), jnp.float32)
    value_grad = jnp.zeros((seq_count, full_len, my_heads, head_dim), jnp.float32)
    query_parts = []
    for block_index, first_row in enumerate(range(0, full_len, block_rows)):
        query_block = queries[:, first_row : first_row + block_rows]
        grad_block = d_heads[:, first_row : first_row + block_rows]
        scores = masked_scores(query_block, key_rows, doc_ids, first_row, block_rows, factor)
        prob_full = jnp.exp(scores - lse_list[block_index])
        prob_low = prob_full.astype(jnp.bfloat16)
        d_probs = jnp.einsum(
            "bqhe,bkhe->bhqk", grad_block, value_rows, preferred_element_type=jnp.float32
        )
        row_delta = jnp.sum(prob_full * d_probs, axis=-1, keepdims=True)
        d_scores = (prob_full * (d_probs - row_delta)).astype(jnp.bfloat16)
        query_parts.append(
            factor
            * jnp.einsum("bhqk,bkhe->bqhe", d_scores, key_rows, preferred_element_type=jnp.float32)
        )
        key_grad = key_grad + factor * jnp.einsum(
            "bhqk,bqhe->bkhe", d_scores, query_block, preferred_element_type=jnp.float32
        )
        value_grad = value_grad + jnp.einsum(
            "bhqk,bqhe->bkhe", prob_low, grad_block, preferred_element_type=jnp.float32
        )
    query_grad = jnp.concatenate(query_parts, axis=1)
    d_packed = jnp.stack([query_grad, key_grad, value_grad], axis=3).astype(jnp.bfloat16)
    d_packed = d_packed.reshape(seq_count, full_len, my_heads * 3 * head_dim)
    d_tokens = lax.all_to_all(d_packed, "seq", split_axis=1, concat_axis=2, tiled=True)
    d_tokens = d_tokens.reshape(token_count, 3 * width)
    qkv_grad = jnp.einsum("td,tc->dc", normed_one, d_tokens, preferred_element_type=jnp.float32)
    column_sums = jnp.sum(d_tokens.astype(jnp.float32), axis=0).reshape(heads_all, 3, head_dim)
    qv_bias_grad = jnp.concatenate([column_sums[:, 0], column_sums[:, 2]], axis=1)
    d_norm_one = jnp.einsum("tc,dc->td", d_tokens, qkv_matrix, preferred_element_type=jnp.float32)
    first_value, first_back = jax.vjp(centred_norm, resid_flat, gain_one)
    d_resid_part, gain_one_grad = first_back(d_norm_one)
    input_grad = (d_middle + d_resid_part).reshape(seq_count, local_len, narrow)
    qkv_share, out_share, fc_share, proj_share = (
        lax.psum_scatter(qkv_grad, "fsdp", scatter_dimension=0, tiled=True),
        lax.psum_scatter(out_weight_part, "fsdp", scatter_dimension=0, tiled=True),
        lax.psum_scatter(fc_grad, "fsdp", scatter_dimension=0, tiled=True),
        lax.psum_scatter(proj_grad, "fsdp", scatter_dimension=0, tiled=True),
    )
    qkv_share, out_share, fc_share, proj_share = (
        lax.psum(qkv_share.astype(jnp.bfloat16), "seq").astype(jnp.float32),
        lax.psum(out_share.astype(jnp.bfloat16), "seq").astype(jnp.float32),
        lax.psum(fc_share.astype(jnp.bfloat16), "seq").astype(jnp.float32),
        lax.psum(proj_share.astype(jnp.bfloat16), "seq").astype(jnp.float32),
    )
    vector_sums = lax.psum(
        (gain_one_grad, qv_bias_grad, out_bias_grad, gain_two_grad, fc_bias_grad, proj_bias_grad),
        ("fsdp", "seq"),
    )
    return (
        output,
        input_grad,
        vector_sums[0],
        qkv_share,
        vector_sums[1],
        out_share,
        vector_sums[2],
        vector_sums[3],
        fc_share,
        vector_sums[4],
        proj_share,
        vector_sums[5],
    )


def solution(mesh):
    return jax.shard_map(
        local,
        mesh=mesh,
        in_specs=(
            P("fsdp", "seq", None),
            P("fsdp", "seq", None),
            P("fsdp", None),
            P(),
            P("fsdp", None),
            P(),
            P("fsdp", None),
            P(),
            P(),
            P("fsdp", None),
            P(),
            P("fsdp", None),
            P(),
        ),
        out_specs=(
            P("fsdp", "seq", None),
            P("fsdp", "seq", None),
            P(),
            P("fsdp", None),
            P(),
            P("fsdp", None),
            P(),
            P(),
            P("fsdp", None),
            P(),
            P("fsdp", None),
            P(),
        ),
        check_vma=False,
    )
```

profile of v0, /device:TPU:0, one launch (start us, length us, event | category | flops | bytes accessed | tf_op | source)
XLA Modules:
  0.0 1041.5 jit_solution(17890892516380688609)
XLA Ops:
  15.6 63.1 %all-gather.5.cloned.1.call-done = bf16[768,2304]{1,0:T(8,128)(2,1)} async-done(((bf16[96,2304]{1,0:T(8,128)(2,1)}), bf16[768,2304]{1,0:T(8,128)(2,1)}) %all-gather.5.cloned.1.call-update) | async-done | bytes 3538960 | tf_op jit(solution)/shard_map/all_gather | solution.py:64
  78.7 6.6 add_convert_fusion
  85.3 9.1 reshape.215
  94.4 7.9 copy.69
  102.3 3.8 all-to-all-start
  109.2 3.8 compare_and_fusion.1
  113.0 34.3 %all-to-all-done = bf16[3,256,4,576]{1,3,0,2:T(8,128)(2,1)S(1)} async-done(((bf16[3,256,4,576]{1,3,0,2:T(8,128)(2,1)}), bf16[3,256,4,576]{1,3,0,2:T(8,128)(2,1)S(1)}, u32[]{:S(2)}, u32[]{:S(2)}) %all-to-all-start) | async-done | bytes 3538976 | tf_op jit(solution)/shard_map/all_to_all | solution.py:79
  147.2 4.5 copy.70
  151.8 6.1 reshape.216
  159.8 9.2 fusion.57
  169.0 10.1 fusion.1
  179.0 9.0 fusion.28
  190.7 10.6 %fusion.58 = (f32[3,3,512]{2,1,0:T(4,128)}, f32[3,3,512,1024]{3,2,1,0:T(8,128)}) fusion(bf16[3,1024,3,3,64]{1,4,3,2,0:T(8,128)(2,1)S(1)} %reshape.216, bf16[3,1024,3,64]{1,3,2,0:T(8,128)(2,1)} %copy-done.13, pred[3,512,1024]{2,1,0:T(8,128)(4,1)} %get-tuple-element.34), kind=kOutput, calls=%fused_computation.122 | convolution fusion | flops 618130944 | bytes 22235136 | tf_op jit(solution)/shard_map/bqhe,bkhe->bhqk/dot_general | solution.py:25
  201.3 10.0 fusion
  211.3 9.0 fusion.29
  225.7 28.3 %all_to_all.60 = bf16[3,1024,192]{2,0,1:T(4,128)(2,1)S(1)} all-to-all(bf16[3,1024,192]{2,0,1:T(4,128)(2,1)S(1)} %pad_maximum_fusion.3), channel_id=1, replica_groups=mesh['fsdp'=8,'seq'=4] {'seq'}, dimensions={1} | all-to-all | bytes 2359296 | tf_op jit(solution)/shard_map/all_to_all | solution.py:106
  256.6 4.0 reshape.217
  265.6 10.9 %fusion.51 = f32[768,3072]{1,0:T(8,128)} fusion(bf16[768,3072]{1,0:T(8,128)(2,1)} %all-gather.9.cloned.1.call-done, f32[768]{0:T(1024)S(1)} %copy-done.25, f32[768]{0:T(1024)S(1)} %fusion.48, f32[768,1]{1,0:T(8,128)} %copy-done.11, f32[768,767]{1,0:T(8,128)} %copy-done.4), kind=kOutput, calls=%fused_computation.117 | convolution fusion | flops 3626237952 | bytes 16521216 | tf_op jit(solution)/shard_map/dot_general | solution.py:112
  276.5 5.5 all-gather.11.cloned.1.call-done
  282.0 13.7 %convert_reduce_fusion = (f32[3072]{0:T(1024)}, bf16[768,3072]{1,0:T(8,128)(2,1)S(1)}) fusion(f32[768,3072]{1,0:T(8,128)} %fusion.51, f32[3072]{0:T(1024)} %param.23, bf16[768,767]{1,0:T(8,128)(2,1)} %bitcast.116, bf16[3072,767]{1,0:T(8,128)(2,1)} %all-gather.11.cloned.1.call-done), kind=kOutput, calls=%fused_computation.27 | convolution fusion | flops 3673420800 | bytes 20070912 | tf_op jit(solution)/shard_map/tc,fc->tf/dot_general | solution.py:126
  295.7 4.8 multiply_reduce_fusion.2
  306.0 4.4 reshape.220
  310.4 3.5 copy.79
  314.0 4.3 all-to-all-start.2
  321.1 4.1 fusion.60
  325.3 8.9 all-to-all-done.2
  334.2 3.2 copy.80
  337.4 3.8 reshape.221
  341.2 8.6 fusion.11
  349.9 15.6 %multiply_reduce_fusion = (f32[3,3,512]{2,1,0:T(4,128)S(1)}, f32[3,3,512,1024]{3,2,1,0:T(8,128)}) fusion(f32[3,3,512,1024]{3,2,1,0:T(8,128)} %get-tuple-element.41, f32[3,3,512]{2,1,0:T(4,128)S(1)} %copy-done.21, bf16[3,1024,3,3,64]{1,4,3,2,0:T(8,128)(2,1)S(1)} %reshape.216, bf16[3,1024,3,64]{1,3,2,0:T(8,128)(2,1)S(1)} %copy-done.8), kind=kOutput, calls=%fused_computation.1 | convolution fusion | flops 618130944 | bytes 39561216 | tf_op jit(solution)/shard_map/bqhe,bkhe->bhqk/dot_general | solution.py:155
  365.5 15.5 %multiply_reduce_fusion.1 = (f32[3,3,512]{2,1,0:T(4,128)S(1)}, f32[3,3,512,1024]{3,2,1,0:T(8,128)}) fusion(f32[3,3,512,1024]{3,2,1,0:T(8,128)} %get-tuple-element.43, f32[3,3,512]{2,1,0:T(4,128)S(1)} %copy-done.22, bf16[3,1024,3,3,64]{1,4,3,2,0:T(8,128)(2,1)S(1)} %reshape.216, bf16[3,1024,3,64]{1,3,2,0:T(8,128)(2,1)S(1)} %copy-done.8), kind=kOutput, calls=%fused_computation.4 | convolution fusion | flops 618130944 | bytes 39561216 | tf_op jit(solution)/shard_map/bqhe,bkhe->bhqk/dot_general | solution.py:155
  381.0 13.1 %multiply_convert_fusion.1 = bf16[3,3,512,1024]{3,2,1,0:T(8,128)(2,1)S(1)} fusion(f32[3,3,512,1024]{3,2,1,0:T(8,128)} %get-tuple-element.48, f32[3,3,512,1024]{3,2,1,0:T(8,128)} %get-tuple-element.43, f32[3,3,512]{2,1,0:T(4,128)S(1)} %get-tuple-element.47, f32[3,3,512]{2,1,0:T(4,128)S(1)} %copy-done.22), kind=kLoop, calls=%fused_computation.3 | loop fusion | flops 18874368 | bytes 47222784 | tf_op jit(solution)/shard_map/convert_element_type | solution.py:159
  399.0 8.3 fusion.24
  407.2 13.1 %multiply_convert_fusion = bf16[3,3,512,1024]{3,2,1,0:T(8,128)(2,1)S(1)} fusion(f32[3,3,512,1024]{3,2,1,0:T(8,128)} %get-tuple-element.50, f32[3,3,512,1024]{3,2,1,0:T(8,128)} %get-tuple-element.41, f32[3,3,512]{2,1,0:T(4,128)S(1)} %get-tuple-element.49, f32[3,3,512]{2,1,0:T(4,128)S(1)} %copy-done.21), kind=kLoop, calls=%fused_computation | loop fusion | flops 18874368 | bytes 47222784 | tf_op jit(solution)/shard_map/convert_element_type | solution.py:159
  426.2 6.2 copy.82
  432.4 63.3 %all_to_all.61 = bf16[3,1024,576]{2,0,1:T(4,128)(2,1)S(1)} all-to-all(bf16[3,1024,576]{2,0,1:T(4,128)(2,1)} %copy.82), channel_id=1, replica_groups=mesh['fsdp'=8,'seq'=4] {'seq'}, dimensions={1} | all-to-all | bytes 7077888 | tf_op jit(solution)/shard_map/all_to_all | solution.py:173
  495.7 6.6 convert_reduce_fusion.1
  502.3 8.0 reshape.222
  510.3 7.6 fusion.49
  519.2 13.5 %fusion.52 = f32[3072,767]{1,0:T(8,128)} fusion(bf16[768,767]{1,0:T(8,128)(2,1)S(1)} %bitcast.117, f32[768,3072]{1,0:T(8,128)} %fusion.51, f32[3072]{0:T(1024)} %param.23), kind=kOutput, calls=%fused_computation.118 | convolution fusion | flops 3642753024 | bytes 20052480 | tf_op jit(solution)/shard_map/tf,tc->fc/dot_general | solution.py:124
  532.8 10.8 %fusion.50 = f32[768,3072]{1,0:T(8,128)} fusion(bf16[768,3072]{1,0:T(8,128)(2,1)} %copy-done.15, f32[768]{0:T(1024)S(1)} %copy-done.25, f32[768]{0:T(1024)S(1)} %fusion.48, f32[768,1]{1,0:T(8,128)} %copy-done.11, f32[768,767]{1,0:T(8,128)} %copy-done.4), kind=kOutput, calls=%fused_computation.116 | convolution fusion | flops 3626237952 | bytes 16521216 | tf_op jit(solution)/shard_map/td,tf->df/dot_general | solution.py:129
  544.8 12.8 %add_convert_fusion.2 = bf16[768,767]{1,0:T(8,128)(2,1)} fusion(f32[768,767]{1,0:T(8,128)} %copy-done.4, bf16[3072,767]{1,0:T(8,128)(2,1)} %all-gather.11.cloned.1.call-done, f32[767]{0:T(1024)S(1)} %copy-done.38, f32[768,3072]{1,0:T(8,128)} %fusion.51, f32[3072]{0:T(1024)} %param.23), kind=kOutput, calls=%fused_computation.55 | convolution fusion | flops 3644520192 | bytes 17699324 | tf_op jit(solution)/shard_map/dot_general | solution.py:114
  560.5 8.2 multiply_reduce_fusion.3
  568.7 39.5 %all-reduce = (f32[768]{0:T(1024)}, f32[12,128]{1,0:T(8,128)}, f32[767]{0:T(1024)}, f32[768]{0:T(1024)}, f32[3072]{0:T(1024)}, /*index=5*/f32[767]{0:T(1024)}) all-reduce(f32[768]{0:T(1024)} %get-tuple-element.14, f32[12,128]{1,0:T(8,128)} %pad_maximum_fusion.5, ...), channel_id=1, replica_groups=mesh['fsdp'=8,'seq'=4] {'fsdp','seq'}, use_global_device_ids=true, to_apply=%region_15.16 | all-reduce | flops 7678 | bytes 61424 | tf_op jit(solution)/shard_map/psum | solution.py:194
  610.6 34.1 %reduce-scatter.5.cloned.1.call-done = f32[96,2304]{1,0:T(8,128)} async-done(((f32[768,2304]{1,0:T(8,128)}), f32[96,2304]{1,0:T(8,128)}) %reduce-scatter.5.cloned.1.call-update) | async-done | bytes 884752 | tf_op jit(solution)/shard_map/reduce_scatter | solution.py:183
  646.6 164.6 %reduce-scatter.11.cloned.1.call-done = f32[384,767]{1,0:T(8,128)} async-done(((f32[3072,767]{1,0:T(8,128)}), f32[384,767]{1,0:T(8,128)}) %reduce-scatter.11.cloned.1.call-update) | async-done | bytes 1178128 | tf_op jit(solution)/shard_map/reduce_scatter | solution.py:186
  813.4 164.5 %reduce-scatter.9.cloned.1.call-done = f32[96,3072]{1,0:T(8,128)} async-done(((f32[768,3072]{1,0:T(8,128)}), f32[96,3072]{1,0:T(8,128)}) %reduce-scatter.9.cloned.1.call-update) | async-done | bytes 1179664 | tf_op jit(solution)/shard_map/reduce_scatter | solution.py:185
  984.6 42.9 %all-reduce.4.cloned.1.call-done = (bf16[96,2304]{1,0:T(8,128)(2,1)}, bf16[96,767]{1,0:T(8,128)(2,1)}, bf16[96,3072]{1,0:T(8,128)(2,1)}, bf16[384,767]{1,0:T(8,128)(2,1)}) async-done(((bf16[96,2304]{1,0:T(8,128)(2,1)}, bf16[96,767]{1,0:T(8,128)(2,1)}, bf16[96,3072]{1,0:T(8,128)(2,1)}, bf16[384,767]{1,0:T(8,128)(2,1)}), (bf16[96,2304]{1,0:T(8,128)(2,1)}, bf16[96,767]{1,0:T(8,128)(2,1)}, ...) | async-done | bytes 1768528 | tf_op jit(solution)/shard_map/psum | solution.py:189
  (164 shorter events, 73.4 us)
Async XLA Ops:
  7.2 4.0 copy-start.18
  7.2 4.9 copy-start.16
  7.2 71.5 %all-gather.5.cloned.1.call-start = ((), (), s32[]{:S(2)}) async-start(), calls=%async_computation.8 | async-start | bytes 3981312 | tf_op jit(solution)/shard_map/all_gather | solution.py:64
  9.4 3.1 copy-start.32
  9.4 251.2 %all-gather.7.cloned.1.call-start = ((), (), s32[]{:S(2)}) async-start(), calls=%async_computation.9 | async-start | bytes 1327104 | tf_op jit(solution)/shard_map/all_gather | solution.py:65
  11.1 254.5 %all-gather.9.cloned.1.call-start = ((), (), s32[]{:S(2)}) async-start(), calls=%async_computation.10 | async-start | bytes 5308416 | tf_op jit(solution)/shard_map/all_gather | solution.py:66
  12.9 65.9 %copy-start.9 = (f32[1,768]{0,1:T(8,128)}, f32[1,768]{0,1:T(8,128)S(1)}, u32[]{:S(2)}) copy-start(f32[1,768]{0,1:T(8,128)S(1)} %copy.93) | copy-start | bytes 9220
  12.9 65.8 %copy-start.26 = (f32[768]{0:T(1024)S(1)}, f32[768]{0:T(1024)}, u32[]{:S(2)}) copy-start(f32[768]{0:T(1024)} %param.16) | copy-start | bytes 9220
  14.5 70.8 %copy-start = (f32[768,767]{1,0:T(8,128)}, f32[768,767]{1,0:T(8,128)S(1)}, u32[]{:S(2)}) copy-start(f32[768,767]{1,0:T(8,128)S(1)} %convert.50) | copy-start | bytes 7068676
  15.6 69.7 %copy-start.23 = (f32[768]{0:T(1024)}, f32[768]{0:T(1024)S(1)}, u32[]{:S(2)}) copy-start(f32[768]{0:T(1024)S(1)} %fusion.47) | copy-start | bytes 9220
  102.3 45.0 %all-to-all-start = ((bf16[3,256,4,576]{1,3,0,2:T(8,128)(2,1)}), bf16[3,256,4,576]{1,3,0,2:T(8,128)(2,1)S(1)}, u32[]{:S(2)}, u32[]{:S(2)}) async-start(bf16[3,256,4,576]{1,3,0,2:T(8,128)(2,1)} %copy.69), calls=%async_computation | async-start | bytes 7077888 | tf_op jit(solution)/shard_map/all_to_all | solution.py:79
  106.1 2.2 copy-start.34
  106.1 175.9 %all-gather.11.cloned.1.call-start = ((), (), s32[]{:S(2)}) async-start(), calls=%async_computation.11 | async-start | bytes 5308416 | tf_op jit(solution)/shard_map/all_gather | solution.py:67
  157.8 1.9 copy-start.17
  158.0 11.0 %copy-start.13 = (bf16[3,1024,3,64]{1,3,2,0:T(8,128)(2,1)}, bf16[3,1024,3,64]{1,3,2,0:T(8,128)(2,1)S(1)}, u32[]{:S(2)}) copy-start(bf16[3,1024,3,64]{1,3,2,0:T(8,128)(2,1)S(1)} %slice_bitcast_fusion.1) | copy-start | bytes 3538948
  254.0 6.6 copy-start.37
  263.8 1.4 copy-start.4
  263.8 1.8 copy-start.25
  264.0 1.5 copy-start.11
  282.0 13.7 %copy-start.5 = (f32[768,767]{1,0:T(8,128)S(1)}, f32[768,767]{1,0:T(8,128)}, u32[]{:S(2)}) copy-start(f32[768,767]{1,0:T(8,128)} %copy-done.4) | copy-start | bytes 7068676
  282.0 13.7 %copy-start.12 = (f32[768,1]{1,0:T(8,128)S(1)}, f32[768,1]{1,0:T(8,128)}, u32[]{:S(2)}) copy-start(f32[768,1]{1,0:T(8,128)} %copy-done.11) | copy-start | bytes 9220
  282.0 13.7 %copy-start.35 = (bf16[768,3072]{1,0:T(8,128)(2,1)S(1)}, bf16[768,3072]{1,0:T(8,128)(2,1)}, u32[]{:S(2)}) copy-start(bf16[768,3072]{1,0:T(8,128)(2,1)} %all-gather.9.cloned.1.call-done) | copy-start | bytes 14155780
  295.7 4.8 copy-start.15
  300.5 1.3 copy-start.6
  301.1 1.7 copy-start.2
  301.8 1.1 copy-start.28
  301.8 2.1 copy-start.36
  314.0 20.2 %all-to-all-start.2 = ((bf16[3,256,4,192]{1,3,0,2:T(8,128)(2,1)}), bf16[3,256,4,192]{1,3,0,2:T(8,128)(2,1)}, u32[]{:S(2)}, u32[]{:S(2)}) async-start(bf16[3,256,4,192]{1,3,0,2:T(8,128)(2,1)} %copy.79), calls=%async_computation.2 | async-start | bytes 2359296 | tf_op jit(solution)/shard_map/all_to_all | solution.py:144
  318.3 290.7 %reduce-scatter.7.cloned.1.call-start = ((), (), s32[]{:S(2)}) async-start(), calls=%async_computation.13 | async-start | bytes 2654208 | tf_op jit(solution)/shard_map/reduce_scatter | solution.py:184
  325.2 319.5 %reduce-scatter.5.cloned.1.call-start = ((), (), s32[]{:S(2)}) async-start(), calls=%async_computation.12 | async-start | bytes 7962624 | tf_op jit(solution)/shard_map/reduce_scatter | solution.py:183
  341.2 8.6 copy-start.8
  341.2 8.7 copy-start.21
  349.9 15.7 %copy-start.22 = (f32[3,3,512]{2,1,0:T(4,128)S(1)}, f32[3,3,512]{2,1,0:T(4,128)}, u32[]{:S(2)}) copy-start(f32[3,3,512]{2,1,0:T(4,128)} %log_add_fusion.1) | copy-start | bytes 55300
  394.1 3.1 copy-start.14
  502.3 8.0 copy-start.1
  502.3 8.0 copy-start.10
  502.3 8.0 copy-start.24
  502.3 8.0 copy-start.27
  518.0 1.3 copy-start.7
  518.0 293.3 %reduce-scatter.11.cloned.1.call-start = ((), (), s32[]{:S(2)}) async-start(), calls=%async_computation.15 | async-start | bytes 10616832 | tf_op jit(solution)/shard_map/reduce_scatter | solution.py:186
  532.7 445.1 %reduce-scatter.9.cloned.1.call-start = ((), (), s32[]{:S(2)}) async-start(), calls=%async_computation.14 | async-start | bytes 10616832 | tf_op jit(solution)/shard_map/reduce_scatter | solution.py:185
  543.6 1.2 copy-start.38
  543.6 484.0 %all-reduce.4.cloned.1.call-start = ((), (), s32[]{:S(2)}) async-start(), calls=%async_computation.16 | async-start | bytes 3538944 | tf_op jit(solution)/shard_map/psum | solution.py:189
  560.5 8.2 copy-start.33
  560.5 47.7 %copy-start.31 = (f32[768]{0:T(1024)S(1)}, f32[768]{0:T(1024)}, u32[]{:S(2)}) copy-start(f32[768]{0:T(1024)} %copy-done.30) | copy-start | bytes 9220
  980.0 2.7 copy-start.3
  980.1 2.7 copy-start.29
  1027.6 5.9 copy-start.20
  (2 other events, 1.9 us)
Sparse Core Ops, SparseCore 0:
  10.8 67.8 all-gather.4
  81.5 39.5 all-gather.6
  123.2 78.6 all-gather.8
  204.0 77.9 all-gather.10
  325.3 67.4 reduce-scatter.6
  518.1 126.5 reduce-scatter.4
  648.7 162.5 reduce-scatter.10
  815.3 162.5 reduce-scatter.8
  981.8 45.7 all-reduce.3
where the time goes:
time: 1050 us; the launch traced here: 1040 us
  waiting for transfers between devices  518 us (49%)
  matrix products  194 us (18%)
  blocking collectives  131 us (12%)
  other arithmetic  96.7 us (9%)
  local copies, waits for them, and re-layouts  78 us (7%)
  between operations  14.8 us (1%)
    reduce_scatter x1, waiting for transfers between devices, local(): lax.psum_scatter(proj_grad, 'fsdp', scatter_dimension=0, tiled=True)  165 us
    reduce_scatter x1, waiting for transfers between devices, local(): lax.psum_scatter(fc_grad, 'fsdp', scatter_dimension=0, tiled=True)  164 us
    all_to_all x1, blocking collectives, local(): lax.all_to_all(d_packed, 'seq', split_axis=1, concat_axis=2, tiled=True)  63.3 us
    all_gather x1, waiting for transfers between devices, local(): lax.all_gather(qkv_weight.astype(jnp.bfloat16), 'fsdp', axis=0, tiled=True)  63.1 us
    psum x1, waiting for transfers between devices, local(): lax.psum(qkv_share.astype(jnp.bfloat16), 'seq').astype(jnp.float32)  42.9 us
    psum x1, blocking collectives, local(): lax.psum((gain_one_grad, qv_bias_grad, out_bias_grad, gain_two_grad, fc_b...  39.5 us
    all_to_all x1, waiting for transfers between devices, local(): lax.all_to_all(packed, 'seq', split_axis=2, concat_axis=1, tiled=True)  34.3 us
    reduce_scatter x1, waiting for transfers between devices, local(): lax.psum_scatter(qkv_grad, 'fsdp', scatter_dimension=0, tiled=True)  34.1 us
  transfers between devices with their start and end apart: 11, of which 8 were waited for; matrix products, arithmetic and copies ran while one was open for 31% of the time, Pallas kernels for 0%

commit v1 on v0

--- a/solution.py
+++ b/solution.py
@@ -186,7 +186,7 @@
         lax.psum_scatter(proj_grad, "fsdp", scatter_dimension=0, tiled=True),
     )
     qkv_share, out_share, fc_share, proj_share = (
-        lax.psum(qkv_share.astype(jnp.bfloat16), "seq").astype(jnp.float32),
+        jnp.sum(lax.all_gather(qkv_share.astype(jnp.bfloat16), "seq"), axis=0).astype(jnp.float32),
         lax.psum(out_share.astype(jnp.bfloat16), "seq").astype(jnp.float32),
         lax.psum(fc_share.astype(jnp.bfloat16), "seq").astype(jnp.float32),
         lax.psum(proj_share.astype(jnp.bfloat16), "seq").astype(jnp.float32),

time: 1050 us -> 932 us (0.89)
  waiting for transfers between devices: 518 us -> 386 us
    reduce_scatter x1, waiting for transfers between devices: 165 us -> 0.01 us  [local(): lax.psum_scatter(proj_grad, 'fsdp', scatter_dimension=0, tiled=True)]
    reduce_scatter x1, waiting for transfers between devices: 34.1 us -> 129 us  [local(): lax.psum_scatter(qkv_grad, 'fsdp', scatter_dimension=0, tiled=True)]
    psum x1, waiting for transfers between devices: 42.9 us -> 0.01 us  [local(): lax.psum(out_share.astype(jnp.bfloat16), 'seq').astype(jnp.float32)]
    reduce_scatter x1, waiting for transfers between devices: 164 us -> 142 us  [local(): lax.psum_scatter(fc_grad, 'fsdp', scatter_dimension=0, tiled=True)]
  transfers between devices with their start and end apart: 11 -> 12, of which waited for: 8 -> 6; matrix products, arithmetic and copies ran while one was open for 31% -> 37% of each run, Pallas kernels for 0% -> 0%
where the time goes in v1:
time: 932 us; the launch traced here: 925 us
  waiting for transfers between devices  386 us (41%)
  matrix products  198 us (21%)
  blocking collectives  133 us (14%)
  other arithmetic  99.6 us (11%)
  local copies, waits for them, and re-layouts  83.2 us (9%)
  between operations  15 us (2%)
    reduce_scatter x1, waiting for transfers between devices, local(): lax.psum_scatter(fc_grad, 'fsdp', scatter_dimension=0, tiled=True)  142 us
    reduce_scatter x1, waiting for transfers between devices, local(): lax.psum_scatter(qkv_grad, 'fsdp', scatter_dimension=0, tiled=True)  129 us
    all_to_all x1, blocking collectives, local(): lax.all_to_all(d_packed, 'seq', split_axis=1, concat_axis=2, tiled=True)  63.7 us
    all_gather x1, waiting for transfers between devices, local(): lax.all_gather(qkv_weight.astype(jnp.bfloat16), 'fsdp', axis=0, tiled=True)  63 us
    psum x1, blocking collectives, local(): lax.psum((gain_one_grad, qv_bias_grad, out_bias_grad, gain_two_grad, fc_b...  41.2 us
    all_to_all x1, waiting for transfers between devices, local(): lax.all_to_all(packed, 'seq', split_axis=2, concat_axis=1, tiled=True)  33.9 us
    dot_general x2, matrix products, local(): jnp.einsum('bqhe,bkhe->bhqk', grad_block, value_rows, preferred_element_t...  31.6 us
    all_to_all x1, blocking collectives, local(): lax.all_to_all(attended, 'seq', split_axis=1, concat_axis=2, tiled=True)  28.4 us
  transfers between devices with their start and end apart: 12, of which 6 were waited for; matrix products, arithmetic and copies ran while one was open for 37% of the time, Pallas kernels for 0%

profile of v1, /device:TPU:0, one launch (start us, length us, event | category | flops | bytes accessed | tf_op | source)
XLA Modules:
  0.0 925.0 jit_solution(14397701955618658779)
XLA Ops:
  15.7 63.0 %all-gather.7.cloned.1.call-done = bf16[768,2304]{1,0:T(8,128)(2,1)} async-done(((bf16[96,2304]{1,0:T(8,128)(2,1)}), bf16[768,2304]{1,0:T(8,128)(2,1)}) %all-gather.7.cloned.1.call-update) | async-done | bytes 3538960 | tf_op jit(solution)/shard_map/all_gather | solution.py:64
  78.7 6.6 add_convert_fusion
  85.3 9.1 reshape.215
  94.4 7.9 copy.69
  102.3 3.8 all-to-all-start
  109.3 4.1 compare_and_fusion.1
  113.4 33.9 %all-to-all-done = bf16[3,256,4,576]{1,3,0,2:T(8,128)(2,1)S(1)} async-done(((bf16[3,256,4,576]{1,3,0,2:T(8,128)(2,1)}), bf16[3,256,4,576]{1,3,0,2:T(8,128)(2,1)S(1)}, u32[]{:S(2)}, u32[]{:S(2)}) %all-to-all-start) | async-done | bytes 3538976 | tf_op jit(solution)/shard_map/all_to_all | solution.py:79
  147.2 4.5 copy.70
  151.7 6.1 reshape.216
  159.8 9.2 fusion.57
  169.0 10.1 %fusion.1 = f32[3,3,512]{2,1,0:T(4,128)} fusion(f32[3,3,512,1024]{3,2,1,0:T(8,128)} %get-tuple-element.40, f32[3,3,512]{2,1,0:T(4,128)} %get-tuple-element.39), kind=kLoop, calls=%fused_computation.13 | loop fusion | flops 9432576 | bytes 18911232 | tf_op jit(solution)/shard_map/reduce_sum | solution.py:98
  179.0 9.0 fusion.28
  190.5 10.6 %fusion.58 = (f32[3,3,512]{2,1,0:T(4,128)}, f32[3,3,512,1024]{3,2,1,0:T(8,128)}) fusion(bf16[3,1024,3,3,64]{1,4,3,2,0:T(8,128)(2,1)S(1)} %reshape.216, bf16[3,1024,3,64]{1,3,2,0:T(8,128)(2,1)} %copy-done.17, pred[3,512,1024]{2,1,0:T(8,128)(4,1)} %get-tuple-element.33), kind=kOutput, calls=%fused_computation.122 | convolution fusion | flops 618130944 | bytes 22235136 | tf_op jit(solution)/shard_map/bqhe,bkhe->bhqk/dot_general | solution.py:25
  201.1 10.0 %fusion = f32[3,3,512]{2,1,0:T(4,128)} fusion(f32[3,3,512,1024]{3,2,1,0:T(8,128)} %get-tuple-element.42, f32[3,3,512]{2,1,0:T(4,128)} %get-tuple-element.41), kind=kLoop, calls=%fused_computation.12 | loop fusion | flops 9432576 | bytes 18911232 | tf_op jit(solution)/shard_map/reduce_sum | solution.py:98
  211.1 9.0 fusion.29
  225.5 28.4 %all_to_all.60 = bf16[3,1024,192]{2,0,1:T(4,128)(2,1)S(1)} all-to-all(bf16[3,1024,192]{2,0,1:T(4,128)(2,1)S(1)} %pad_maximum_fusion.3), channel_id=1, replica_groups=mesh['fsdp'=8,'seq'=4] {'seq'}, dimensions={1} | all-to-all | bytes 2359296 | tf_op jit(solution)/shard_map/all_to_all | solution.py:106
  256.5 4.0 reshape.217
  265.4 10.8 %fusion.51 = f32[768,3072]{1,0:T(8,128)} fusion(bf16[768,3072]{1,0:T(8,128)(2,1)} %all-gather.11.cloned.1.call-done, f32[768]{0:T(1024)S(1)} %copy-done.33, f32[768]{0:T(1024)S(1)} %fusion.48, f32[768,1]{1,0:T(8,128)} %copy-done.14, f32[768,767]{1,0:T(8,128)} %copy-done.6), kind=kOutput, calls=%fused_computation.117 | convolution fusion | flops 3626237952 | bytes 16521216 | tf_op jit(solution)/shard_map/dot_general | solution.py:112
  276.3 5.7 all-gather.13.cloned.1.call-done
  282.0 13.9 %convert_reduce_fusion = (f32[3072]{0:T(1024)}, bf16[768,3072]{1,0:T(8,128)(2,1)S(1)}) fusion(f32[768,3072]{1,0:T(8,128)} %fusion.51, f32[3072]{0:T(1024)} %param.23, bf16[768,767]{1,0:T(8,128)(2,1)} %bitcast.119, bf16[3072,767]{1,0:T(8,128)(2,1)} %all-gather.13.cloned.1.call-done), kind=kOutput, calls=%fused_computation.27 | convolution fusion | flops 3673420800 | bytes 20070912 | tf_op jit(solution)/shard_map/tc,fc->tf/dot_general | solution.py:126
  295.9 4.8 multiply_reduce_fusion.2
  306.7 13.4 %fusion.52 = f32[3072,767]{1,0:T(8,128)} fusion(bf16[768,767]{1,0:T(8,128)(2,1)} %bitcast.120, f32[768,3072]{1,0:T(8,128)} %fusion.51, f32[3072]{0:T(1024)} %param.23), kind=kOutput, calls=%fused_computation.118 | convolution fusion | flops 3642753024 | bytes 20052480 | tf_op jit(solution)/shard_map/tf,tc->fc/dot_general | solution.py:124
  320.3 10.8 %fusion.50 = f32[768,3072]{1,0:T(8,128)} fusion(bf16[768,3072]{1,0:T(8,128)(2,1)} %copy-done.19, f32[768]{0:T(1024)S(1)} %copy-done.33, f32[768]{0:T(1024)S(1)} %fusion.48, f32[768,1]{1,0:T(8,128)} %copy-done.14, f32[768,767]{1,0:T(8,128)} %copy-done.6), kind=kOutput, calls=%fused_computation.116 | convolution fusion | flops 3626237952 | bytes 16521216 | tf_op jit(solution)/shard_map/td,tf->df/dot_general | solution.py:129
  331.1 3.8 convolution_convert_fusion
  334.9 4.4 reshape.220
  339.3 3.5 copy.79
  342.9 4.3 all-to-all-start.2
  350.2 12.9 %all-to-all-done.2 = bf16[3,256,4,192]{1,3,0,2:T(8,128)(2,1)} async-done(((bf16[3,256,4,192]{1,3,0,2:T(8,128)(2,1)}), bf16[3,256,4,192]{1,3,0,2:T(8,128)(2,1)}, u32[]{:S(2)}, u32[]{:S(2)}) %all-to-all-start.2) | async-done | bytes 1179680 | tf_op jit(solution)/shard_map/all_to_all | solution.py:144
  366.3 3.4 reshape.221
  369.7 16.0 %multiply_reduce_fusion = (f32[3,3,512]{2,1,0:T(4,128)S(1)}, f32[3,3,512,1024]{3,2,1,0:T(8,128)}) fusion(f32[3,3,512,1024]{3,2,1,0:T(8,128)} %get-tuple-element.40, f32[3,3,512]{2,1,0:T(4,128)} %log_add_fusion, bf16[3,1024,3,3,64]{1,4,3,2,0:T(8,128)(2,1)S(1)} %reshape.216, bf16[3,1024,3,64]{1,3,2,0:T(8,128)(2,1)} %reshape.221), kind=kOutput, calls=%fused_computation.1 | convolution fusion | flops 618130944 | bytes 39561216 | tf_op jit(solution)/shard_map/bqhe,bkhe->bhqk/dot_general | solution.py:155
  385.7 13.0 %multiply_convert_fusion = bf16[3,3,512,1024]{3,2,1,0:T(8,128)(2,1)S(1)} fusion(f32[3,3,512,1024]{3,2,1,0:T(8,128)} %get-tuple-element.49, f32[3,3,512,1024]{3,2,1,0:T(8,128)} %get-tuple-element.40, f32[3,3,512]{2,1,0:T(4,128)S(1)} %get-tuple-element.48, f32[3,3,512]{2,1,0:T(4,128)S(1)} %copy-done.27), kind=kLoop, calls=%fused_computation | loop fusion | flops 18874368 | bytes 47222784 | tf_op jit(solution)/shard_map/convert_element_type | solution.py:159
  398.7 3.6 copy-done
  405.4 15.6 %multiply_reduce_fusion.1 = (f32[3,3,512]{2,1,0:T(4,128)S(1)}, f32[3,3,512,1024]{3,2,1,0:T(8,128)}) fusion(f32[3,3,512,1024]{3,2,1,0:T(8,128)} %get-tuple-element.42, f32[3,3,512]{2,1,0:T(4,128)S(1)} %copy-done.29, bf16[3,1024,3,3,64]{1,4,3,2,0:T(8,128)(2,1)S(1)} %reshape.216, bf16[3,1024,3,64]{1,3,2,0:T(8,128)(2,1)S(1)} %copy-done.10), kind=kOutput, calls=%fused_computation.4 | convolution fusion | flops 618130944 | bytes 39561216 | tf_op jit(solution)/shard_map/bqhe,bkhe->bhqk/dot_general | solution.py:155
  421.0 13.7 %multiply_convert_fusion.1 = bf16[3,3,512,1024]{3,2,1,0:T(8,128)(2,1)S(1)} fusion(f32[3,3,512,1024]{3,2,1,0:T(8,128)} %get-tuple-element.47, f32[3,3,512,1024]{3,2,1,0:T(8,128)} %get-tuple-element.42, f32[3,3,512]{2,1,0:T(4,128)S(1)} %get-tuple-element.46, f32[3,3,512]{2,1,0:T(4,128)S(1)} %copy-done.29), kind=kLoop, calls=%fused_computation.3 | loop fusion | flops 18874368 | bytes 47222784 | tf_op jit(solution)/shard_map/convert_element_type | solution.py:159
  442.0 5.7 fusion.42
  447.7 6.8 fusion.23
  454.6 3.5 fusion.11
  458.2 8.8 fusion.24
  467.9 6.3 copy.82
  474.1 63.7 %all_to_all.61 = bf16[3,1024,576]{2,0,1:T(4,128)(2,1)S(1)} all-to-all(bf16[3,1024,576]{2,0,1:T(4,128)(2,1)} %copy.82), channel_id=1, replica_groups=mesh['fsdp'=8,'seq'=4] {'seq'}, dimensions={1} | all-to-all | bytes 7077888 | tf_op jit(solution)/shard_map/all_to_all | solution.py:173
  537.8 6.7 convert_reduce_fusion.1
  544.6 8.0 reshape.222
  552.6 7.6 fusion.49
  564.2 142.0 %reduce-scatter.9.cloned.1.call-done = f32[96,3072]{1,0:T(8,128)} async-done(((f32[768,3072]{1,0:T(8,128)}), f32[96,3072]{1,0:T(8,128)}) %reduce-scatter.9.cloned.1.call-update) | async-done | bytes 1179664 | tf_op jit(solution)/shard_map/reduce_scatter | solution.py:185
  709.5 128.6 %reduce-scatter.5.cloned.1.call-done = f32[96,2304]{1,0:T(8,128)} async-done(((f32[768,2304]{1,0:T(8,128)}), f32[96,2304]{1,0:T(8,128)}) %reduce-scatter.5.cloned.1.call-update) | async-done | bytes 884752 | tf_op jit(solution)/shard_map/reduce_scatter | solution.py:183
  840.1 12.6 %add_convert_fusion.2 = bf16[768,767]{1,0:T(8,128)(2,1)} fusion(f32[768,767]{1,0:T(8,128)} %copy-done.6, bf16[3072,767]{1,0:T(8,128)(2,1)} %all-gather.13.cloned.1.call-done, f32[767]{0:T(1024)S(1)} %copy-done.42, f32[768,3072]{1,0:T(8,128)} %fusion.51, f32[3072]{0:T(1024)} %param.23), kind=kOutput, calls=%fused_computation.55 | convolution fusion | flops 3644520192 | bytes 17699324 | tf_op jit(solution)/shard_map/dot_general | solution.py:114
  855.6 8.2 multiply_reduce_fusion.3
  863.8 41.2 %all-reduce = (f32[768]{0:T(1024)}, f32[12,128]{1,0:T(8,128)}, f32[767]{0:T(1024)}, f32[768]{0:T(1024)}, f32[3072]{0:T(1024)}, /*index=5*/f32[767]{0:T(1024)}) all-reduce(f32[768]{0:T(1024)} %get-tuple-element.14, f32[12,128]{1,0:T(8,128)} %pad_maximum_fusion.5, ...), channel_id=1, replica_groups=mesh['fsdp'=8,'seq'=4] {'fsdp','seq'}, use_global_device_ids=true, to_apply=%region_15.16 | all-reduce | flops 7678 | bytes 61424 | tf_op jit(solution)/shard_map/psum | solution.py:194
  (187 shorter events, 77.4 us)
Async XLA Ops:
  7.2 4.0 copy-start.23
  7.2 4.9 copy-start.20
  7.2 71.5 %all-gather.7.cloned.1.call-start = ((), (), s32[]{:S(2)}) async-start(), calls=%async_computation.8 | async-start | bytes 3981312 | tf_op jit(solution)/shard_map/all_gather | solution.py:64
  9.4 3.1 copy-start.38
  9.4 251.1 %all-gather.9.cloned.1.call-start = ((), (), s32[]{:S(2)}) async-start(), calls=%async_computation.9 | async-start | bytes 1327104 | tf_op jit(solution)/shard_map/all_gather | solution.py:65
  11.1 254.3 %all-gather.11.cloned.1.call-start = ((), (), s32[]{:S(2)}) async-start(), calls=%async_computation.10 | async-start | bytes 5308416 | tf_op jit(solution)/shard_map/all_gather | solution.py:66
  12.9 65.9 %copy-start.12 = (f32[1,768]{0,1:T(8,128)}, f32[1,768]{0,1:T(8,128)S(1)}, u32[]{:S(2)}) copy-start(f32[1,768]{0,1:T(8,128)S(1)} %copy.93) | copy-start | bytes 9220
  12.9 65.8 %copy-start.34 = (f32[768]{0:T(1024)S(1)}, f32[768]{0:T(1024)}, u32[]{:S(2)}) copy-start(f32[768]{0:T(1024)} %param.16) | copy-start | bytes 9220
  14.5 70.8 %copy-start.2 = (f32[768,767]{1,0:T(8,128)}, f32[768,767]{1,0:T(8,128)S(1)}, u32[]{:S(2)}) copy-start(f32[768,767]{1,0:T(8,128)S(1)} %convert.51) | copy-start | bytes 7068676
  15.7 69.6 %copy-start.31 = (f32[768]{0:T(1024)}, f32[768]{0:T(1024)S(1)}, u32[]{:S(2)}) copy-start(f32[768]{0:T(1024)S(1)} %fusion.47) | copy-start | bytes 9220
  102.3 45.0 %all-to-all-start = ((bf16[3,256,4,576]{1,3,0,2:T(8,128)(2,1)}), bf16[3,256,4,576]{1,3,0,2:T(8,128)(2,1)S(1)}, u32[]{:S(2)}, u32[]{:S(2)}) async-start(bf16[3,256,4,576]{1,3,0,2:T(8,128)(2,1)} %copy.69), calls=%async_computation | async-start | bytes 7077888 | tf_op jit(solution)/shard_map/all_to_all | solution.py:79
  106.1 175.9 %all-gather.13.cloned.1.call-start = ((), (), s32[]{:S(2)}) async-start(), calls=%async_computation.11 | async-start | bytes 5308416 | tf_op jit(solution)/shard_map/all_gather | solution.py:67
  108.4 451.9 %reduce-scatter.7.cloned.1.call-start = ((), (), s32[]{:S(2)}) async-start(), calls=%async_computation.13 | async-start | bytes 2654208 | tf_op jit(solution)/shard_map/reduce_scatter | solution.py:184
  157.9 11.0 %copy-start.17 = (bf16[3,1024,3,64]{1,3,2,0:T(8,128)(2,1)}, bf16[3,1024,3,64]{1,3,2,0:T(8,128)(2,1)S(1)}, u32[]{:S(2)}) copy-start(bf16[3,1024,3,64]{1,3,2,0:T(8,128)(2,1)S(1)} %slice_bitcast_fusion.1) | copy-start | bytes 3538948
  253.8 6.6 copy-start.41
  282.0 13.9 %copy-start.7 = (f32[768,767]{1,0:T(8,128)S(1)}, f32[768,767]{1,0:T(8,128)}, u32[]{:S(2)}) copy-start(f32[768,767]{1,0:T(8,128)} %copy-done.6) | copy-start | bytes 7068676
  282.0 13.9 %copy-start.15 = (f32[768,1]{1,0:T(8,128)S(1)}, f32[768,1]{1,0:T(8,128)}, u32[]{:S(2)}) copy-start(f32[768,1]{1,0:T(8,128)} %copy-done.14) | copy-start | bytes 9220
  282.0 13.9 %copy-start.40 = (bf16[768,3072]{1,0:T(8,128)(2,1)S(1)}, bf16[768,3072]{1,0:T(8,128)(2,1)}, u32[]{:S(2)}) copy-start(bf16[768,3072]{1,0:T(8,128)(2,1)} %all-gather.11.cloned.1.call-done) | copy-start | bytes 14155780
  295.9 4.8 copy-start.19
  306.6 255.3 %reduce-scatter.11.cloned.1.call-start = ((), (), s32[]{:S(2)}) async-start(), calls=%async_computation.15 | async-start | bytes 10616832 | tf_op jit(solution)/shard_map/reduce_scatter | solution.py:186
  320.1 386.1 %reduce-scatter.9.cloned.1.call-start = ((), (), s32[]{:S(2)}) async-start(), calls=%async_computation.14 | async-start | bytes 10616832 | tf_op jit(solution)/shard_map/reduce_scatter | solution.py:185
  342.9 20.2 %all-to-all-start.2 = ((bf16[3,256,4,192]{1,3,0,2:T(8,128)(2,1)}), bf16[3,256,4,192]{1,3,0,2:T(8,128)(2,1)}, u32[]{:S(2)}, u32[]{:S(2)}) async-start(bf16[3,256,4,192]{1,3,0,2:T(8,128)(2,1)} %copy.79), calls=%async_computation.2 | async-start | bytes 2359296 | tf_op jit(solution)/shard_map/all_to_all | solution.py:144
  347.2 490.8 %reduce-scatter.5.cloned.1.call-start = ((), (), s32[]{:S(2)}) async-start(), calls=%async_computation.12 | async-start | bytes 7962624 | tf_op jit(solution)/shard_map/reduce_scatter | solution.py:183
  369.7 16.0 %copy-start.27 = (f32[3,3,512]{2,1,0:T(4,128)S(1)}, f32[3,3,512]{2,1,0:T(4,128)}, u32[]{:S(2)}) copy-start(f32[3,3,512]{2,1,0:T(4,128)} %log_add_fusion) | copy-start | bytes 55300
  398.7 3.7 copy-start
  402.4 3.1 copy-start.10
  402.4 3.1 copy-start.29
  434.7 4.8 copy-start.1
  434.7 19.8 %slice-start = ((s8[18874368]{0:T(1024)(128)(4,1)}), s8[4194304]{0:T(1024)(128)(4,1)S(1)}, s32[]{:S(2)}) async-start(s8[18874368]{0:T(1024)(128)(4,1)} %bitcast.114), calls=%async_computation.18 | async-start | bytes 8388608
  434.7 19.8 %slice-start.1 = ((s8[18874368]{0:T(1024)(128)(4,1)}), s8[4194304]{0:T(1024)(128)(4,1)S(1)}, s32[]{:S(2)}) async-start(s8[18874368]{0:T(1024)(128)(4,1)} %bitcast.114), calls=%async_computation.19 | async-start | bytes 8388608
  442.0 12.6 %slice-start.2 = ((s8[18874368]{0:T(1024)(128)(4,1)}), s8[4194304]{0:T(1024)(128)(4,1)S(1)}, s32[]{:S(2)}) async-start(s8[18874368]{0:T(1024)(128)(4,1)} %bitcast.114), calls=%async_computation.20 | async-start | bytes 8388608
  442.0 12.6 %slice-start.3 = ((s8[18874368]{0:T(1024)(128)(4,1)}), s8[4194304]{0:T(1024)(128)(4,1)S(1)}, s32[]{:S(2)}) async-start(s8[18874368]{0:T(1024)(128)(4,1)} %bitcast.114), calls=%async_computation.21 | async-start | bytes 8388608
  447.6 6.9 slice-start.4
  447.6 6.9 copy-start.11
  447.7 6.9 copy-start.28
  454.6 3.5 copy-start.30
  458.1 8.8 copy-start.16
  458.1 8.8 copy-start.21
  544.6 8.0 copy-start.3
  544.6 8.0 copy-start.13
  544.6 8.0 copy-start.32
  544.6 8.0 copy-start.35
  560.3 350.0 %all-reduce.4.cloned.1.call-start = ((), (), s32[]{:S(2)}) async-start(), calls=%async_computation.17 | async-start | bytes 2654208 | tf_op jit(solution)/shard_map/psum | solution.py:190
  562.0 146.7 %copy-start.9 = (bf16[3,256,767]{2,1,0:T(8,128)(2,1)S(1)}, bf16[3,256,767]{2,1,0:T(8,128)(2,1)}, u32[]{:S(2)}) copy-start(bf16[3,256,767]{2,1,0:T(8,128)(2,1)} %param.14) | copy-start | bytes 3534340
  708.4 131.7 %copy-start.42 = (f32[767]{0:T(1024)S(1)}, f32[767]{0:T(1024)}, u32[]{:S(2)}) copy-start(f32[767]{0:T(1024)} %param.25) | copy-start | bytes 9208
  708.4 206.8 %all-gather.15.cloned.1.call-start = ((), (), s32[]{:S(2)}) async-start(), calls=%async_computation.16 | async-start | bytes 2211840 | tf_op jit(solution)/shard_map/all_gather | solution.py:189
  855.6 49.4 %copy-start.37 = (f32[768]{0:T(1024)S(1)}, f32[768]{0:T(1024)}, u32[]{:S(2)}) copy-start(f32[768]{0:T(1024)} %copy-done.36) | copy-start | bytes 9220
  910.3 3.9 copy-start.26
  (12 other events, 21.1 us)
Sparse Core Ops, SparseCore 0:
  10.8 67.8 all-gather.6
  81.5 39.5 all-gather.8
  123.2 78.6 all-gather.10
  204.0 78.0 all-gather.12
  306.7 67.2 reduce-scatter.6
  377.5 162.4 reduce-scatter.10
  543.6 162.5 reduce-scatter.8
  709.9 128.0 reduce-scatter.4
  841.9 39.4 all-reduce.3
  882.9 20.8 all-gather.14
